TPU v7x, 256 devices: a whole 4x4x8 slice. The times are simulated.
256 devices in a mesh: row: 8 (over y, core), col: 32 (over x, z).
Axes of the slice: x: 4, y: 4, z: 8, core: 2. Of those that a mesh axis runs over, the one named last changes fastest.
Arguments:
- tokens: bfloat16 [2048, 6144], P('row', 'col'), may hold values from -6 to 6
- cotangent: bfloat16 [2048, 6144], P('row', 'col'), may hold values from -6 to 6
- w_expand: bfloat16 [6144, 12288], P('row', 'col'), may hold values from -0.078125 to 0.078125
- w_reduce: bfloat16 [6144, 12288], P('row', 'col'), may hold values from -0.0546875 to 0.0546875
- expand_mean: bfloat16 [6144, 12288], P('row', 'col'), may hold values from -1 to 1
- expand_mean_scale: float32 [24, 12288], P('row', 'col'), may hold values from 4 to 16
- expand_var: bfloat16 [6144, 12288], P('row', 'col'), may hold values from 0.049804688 to 1
- expand_var_scale: float32 [24, 12288], P('row', 'col'), may hold values from 4 to 16
- reduce_mean: bfloat16 [6144, 12288], P('row', 'col'), may hold values from -1 to 1
- reduce_mean_scale: float32 [24, 12288], P('row', 'col'), may hold values from 4 to 16
- reduce_var: bfloat16 [6144, 12288], P('row', 'col'), may hold values from 0.049804688 to 1
- reduce_var_scale: float32 [24, 12288], P('row', 'col'), may hold values from 4 to 16
Outputs:
- grad_tokens: bfloat16 [2048, 6144], P('row', 'col')
- new_expand: bfloat16 [6144, 12288], P('row', 'col')
- expand_mean_next: bfloat16 [6144, 12288], P('row', 'col')
- expand_mean_scale_next: float32 [24, 12288], P('row', 'col')
- expand_var_next: bfloat16 [6144, 12288], P('row', 'col')
- expand_var_scale_next: float32 [24, 12288], P('row', 'col')
- new_reduce: bfloat16 [6144, 12288], P('row', 'col')
- reduce_mean_next: bfloat16 [6144, 12288], P('row', 'col')
- reduce_mean_scale_next: float32 [24, 12288], P('row', 'col')
- reduce_var_next: bfloat16 [6144, 12288], P('row', 'col')
- reduce_var_scale_next: float32 [24, 12288], P('row', 'col')
All inputs are finite; a program needn't handle non-finite values.
Results may differ from a plain program's by a relative error of at most 0.0049.
Values may be sent and summed in bfloat16 or wider, within the bound.
No kernel may reach another device: no remote copies, remote signals or barrier semaphores. Data moves between devices by JAX's collectives and lax.ppermute only.
A program may use at most 128 MiB of HBM per device.

v0:
```python
import jax
import jax.numpy as jnp
from jax import lax
from jax.sharding import PartitionSpec as P

STEP = 10
beta_one = 0.9
beta_two = 0.999
adam_eps = 1e-08
learn_rate = 0.001
decay_rate = 0.1
scale_eps = 1e-06


def gelu_pair(pre_act):
    cdf_part = 0.5 * (1.0 + lax.erf(pre_act * 0.7071067811865476))
    slope = cdf_part + pre_act * jnp.exp(-0.5 * pre_act * pre_act) * 0.3989422804014327
    return (pre_act * cdf_part, slope)


def spread_scale(values, scale):
    blocks = scale.shape[0]
    shaped = values.reshape(blocks, values.shape[0] // blocks, values.shape[1])
    return (shaped * scale[:, None, :]).reshape(values.shape)


def block_max(values, blocks):
    shaped = values.reshape(blocks, values.shape[0] // blocks, values.shape[1])
    return jnp.max(jnp.abs(shaped), axis=1) + scale_eps


def adam_step(weight, grad_w, mean_q, mean_scale, var_q, var_scale):
    blocks = mean_scale.shape[0]
    mean_new = (
        beta_one * spread_scale(mean_q.astype(jnp.float32), mean_scale) + (1.0 - beta_one) * grad_w
    )
    var_new = (
        beta_two * spread_scale(var_q.astype(jnp.float32), var_scale)
        + (1.0 - beta_two) * grad_w * grad_w
    )
    mean_hat = mean_new / (1.0 - beta_one**STEP)
    var_hat = var_new / (1.0 - beta_two**STEP)
    old_weight = weight.astype(jnp.float32)
    new_weight = (
        old_weight
        - learn_rate * (mean_hat / (jnp.sqrt(var_hat) + adam_eps) + decay_rate * old_weight)
    ).astype(jnp.bfloat16)
    mean_scale_next = block_max(mean_new, blocks)
    var_scale_next = block_max(var_new, blocks)
    mean_next = spread_scale(mean_new, 1.0 / mean_scale_next).astype(jnp.bfloat16)
    var_next = spread_scale(var_new, 1.0 / var_scale_next).astype(jnp.bfloat16)
    return (new_weight, mean_next, mean_scale_next, var_next, var_scale_next)


def contract_first(left, right):
    return lax.dot_general(
        left, right, (((0,), (0,)), ((), ())), preferred_element_type=jnp.float32
    )


def local(
    tokens,
    cotangent,
    w_expand,
    w_reduce,
    expand_mean,
    expand_mean_scale,
    expand_var,
    expand_var_scale,
    reduce_mean,
    reduce_mean_scale,
    reduce_var,
    reduce_var_scale,
):
    token_rows, cot_rows = (
        lax.all_gather(tokens, "col", axis=1, tiled=True),
        lax.all_gather(cotangent, "col", axis=1, tiled=True),
    )
    input_whole, cot_whole = (
        lax.all_to_all(token_rows, "row", split_axis=1, concat_axis=0, tiled=True),
        lax.all_to_all(cot_rows, "row", split_axis=1, concat_axis=0, tiled=True),
    )
    up_panel, down_panel = (
        lax.all_gather(w_expand, "row", axis=0, tiled=True),
        lax.all_gather(w_reduce, "row", axis=0, tiled=True),
    )
    pre_act = jnp.dot(token_rows, up_panel, preferred_element_type=jnp.float32)
    act_grad = jnp.dot(cot_rows, down_panel, preferred_element_type=jnp.float32)
    activated, slope = gelu_pair(pre_act)
    activated = activated.astype(jnp.bfloat16)
    pre_grad = (act_grad * slope).astype(jnp.bfloat16)
    grad_cols = lax.psum_scatter(
        lax.dot_general(
            up_panel, pre_grad, (((1,), (1,)), ((), ())), preferred_element_type=jnp.float32
        ),
        "col",
        scatter_dimension=0,
        tiled=True,
    )
    grad_tokens = grad_cols.T.astype(jnp.bfloat16)
    grad_expand = contract_first(input_whole, lax.all_gather(pre_grad, "row", axis=0, tiled=True))
    grad_reduce = contract_first(cot_whole, lax.all_gather(activated, "row", axis=0, tiled=True))
    first = adam_step(
        w_expand, grad_expand, expand_mean, expand_mean_scale, expand_var, expand_var_scale
    )
    second = adam_step(
        w_reduce, grad_reduce, reduce_mean, reduce_mean_scale, reduce_var, reduce_var_scale
    )
    return (
        grad_tokens,
        first[0],
        first[1],
        first[2],
        first[3],
        first[4],
        second[0],
        second[1],
        second[2],
        second[3],
        second[4],
    )


def solution(mesh):
    placed = (
        P("row", "col"),
        P("row", "col"),
        P("row", "col"),
        P("row", "col"),
        P("row", "col"),
        P("row", "col"),
        P("row", "col"),
        P("row", "col"),
        P("row", "col"),
        P("row", "col"),
        P("row", "col"),
        P("row", "col"),
    )
    return jax.shard_map(
        local,
        mesh=mesh,
        in_specs=placed,
        out_specs=(
            P("row", "col"),
            P("row", "col"),
            P("row", "col"),
            P("row", "col"),
            P("row", "col"),
            P("row", "col"),
            P("row", "col"),
            P("row", "col"),
            P("row", "col"),
            P("row", "col"),
            P("row", "col"),
        ),
        check_vma=False,
    )
```

profile of v0, /device:TPU:8, one launch (start us, length us, event | category | flops | bytes accessed | tf_op | source)
XLA Modules:
  0.0 555.6 jit_solution(1710327823756502407)
XLA Ops:
  10.0 82.9 %all-gather.11.cloned.1.call-done = bf16[256,6144]{0,1:T(8,128)(2,1)} async-done(((bf16[256,192]{0,1:T(8,128)(2,1)}), bf16[256,6144]{0,1:T(8,128)(2,1)}) %all-gather.11.cloned.1.call-update) | async-done | bytes 3145744 | tf_op jit(solution)/shard_map/all_gather | solution.py:76
  92.9 34.3 %all-gather.13.cloned.1.call-done = bf16[6144,384]{1,0:T(8,128)(2,1)} async-done(((bf16[768,384]{1,0:T(8,128)(2,1)}), bf16[6144,384]{1,0:T(8,128)(2,1)}) %all-gather.13.cloned.1.call-update) | async-done | bytes 4718608 | tf_op jit(solution)/shard_map/all_gather | solution.py:84
  127.2 5.8 %multiply_convert_fusion.4 = (bf16[256,384]{1,0:T(8,128)(2,1)}, f32[256,384]{1,0:T(8,128)S(1)}) fusion(bf16[256,6144]{0,1:T(8,128)(2,1)} %all-gather.11.cloned.1.call-done, bf16[6144,384]{1,0:T(8,128)(2,1)} %all-gather.13.cloned.1.call-done), kind=kOutput, calls=%fused_computation.30 | convolution fusion | flops 1208451072 | bytes 8454144 | tf_op jit(solution)/shard_map/dot_general | solution.py:87
  133.1 77.2 %all-gather.7.cloned.1.call-done = bf16[256,6144]{0,1:T(8,128)(2,1)} async-done(((bf16[256,192]{0,1:T(8,128)(2,1)}), bf16[256,6144]{0,1:T(8,128)(2,1)}) %all-gather.7.cloned.1.call-update) | async-done | bytes 3145744 | tf_op jit(solution)/shard_map/all_gather | solution.py:77
  210.2 34.2 %all-gather.9.cloned.1.call-done = bf16[6144,384]{1,0:T(8,128)(2,1)} async-done(((bf16[768,384]{1,0:T(8,128)(2,1)}), bf16[6144,384]{1,0:T(8,128)(2,1)}) %all-gather.9.cloned.1.call-update) | async-done | bytes 4718608 | tf_op jit(solution)/shard_map/all_gather | solution.py:85
  244.4 5.9 %fusion.8 = bf16[256,384]{1,0:T(8,128)(2,1)} fusion(bf16[256,6144]{0,1:T(8,128)(2,1)} %all-gather.7.cloned.1.call-done, bf16[6144,384]{1,0:T(8,128)(2,1)} %all-gather.9.cloned.1.call-done, f32[256,384]{1,0:T(8,128)S(1)} %get-tuple-element.82), kind=kOutput, calls=%fused_computation.24 | convolution fusion | flops 1208942592 | bytes 8454144 | tf_op jit(solution)/shard_map/dot_general | solution.py:88
  250.9 7.0 %convolution_bitcast_fusion = f32[6144,256]{0,1:T(8,128)} fusion(bf16[256,384]{1,0:T(8,128)(2,1)} %fusion.8, bf16[6144,384]{1,0:T(8,128)(2,1)} %all-gather.13.cloned.1.call-done), kind=kOutput, calls=%fused_computation | convolution fusion | flops 1207959552 | bytes 11206656 | tf_op jit(solution)/shard_map/dot_general | solution.py:93
  257.9 6.6 %copy.123 = f32[6144,256]{1,0:T(8,128)} copy(f32[6144,256]{0,1:T(8,128)} %convolution_bitcast_fusion) | data formatting | bytes 12582912
  266.4 49.7 %all_to_all.38 = bf16[256,8,768]{0,2,1:T(8,128)(2,1)} all-to-all(bf16[256,8,768]{0,2,1:T(8,128)(2,1)S(1)} %bitcast.38), channel_id=1, replica_groups=mesh['row'=8,'col'=32] {'row'}, dimensions={1} | all-to-all | bytes 6291456 | tf_op jit(solution)/shard_map/all_to_all | solution.py:80
  316.1 4.0 all-to-all-start.1
  320.2 2.1 copy.96
  325.5 2.7 copy.101
  329.3 2.7 copy.98
  332.0 2.1 copy.100
  337.4 2.7 copy.108
  341.2 2.7 copy.111
  343.8 2.1 copy.107
  346.0 2.1 copy.110
  348.1 4.7 copy.99
  352.8 4.3 all-to-all-done.1
  357.1 2.9 copy.109
  360.0 6.3 %fusion.18 = (f32[768,384]{0,1:T(8,128)}, f32[768,384]{0,1:T(8,128)S(1)}, f32[768,384]{0,1:T(8,128)S(1)}, f32[768,384]{0,1:T(8,128)S(1)}) fusion(f32[768,384]{0,1:T(8,128)} %copy.98, bf16[768,384]{0,1:T(8,128)(2,1)} %copy.97, f32[768,384]{0,1:T(8,128)} %copy.101, bf16[768,384]{0,1:T(8,128)(2,1)} %copy.100, ...), kind=kOutput, calls=%fused_computation.44 | convolution fusion | flops 1211793408 | bytes 12976128 | tf_op jit(solution)/shard_map/dot_general | solution.py:56
  366.3 2.7 copy.102
  377.8 2.7 copy.105
  380.5 3.5 multiply_convert_fusion.2
  384.0 2.3 copy.117
  388.4 2.1 copy.119
  390.5 6.4 %fusion.15 = (f32[768,384]{0,1:T(8,128)}, f32[768,384]{0,1:T(8,128)}, f32[768,384]{0,1:T(8,128)}, f32[768,384]{0,1:T(8,128)}) fusion(f32[768,384]{0,1:T(8,128)} %copy.108, bf16[768,384]{0,1:T(8,128)(2,1)} %copy.107, f32[768,384]{0,1:T(8,128)} %copy.111, bf16[768,384]{0,1:T(8,128)(2,1)} %copy.110, bf16[2048,384]{1,0:T(8,128)(2,1)} %all-gather.17.cloned.1.call-done, ...), kind=kOutput, calls=%fused_computation.42 | convolution fusion | flops 1211793408 | bytes 12976128 | tf_op jit(solution)/shard_map/dot_general | solution.py:56
  402.5 2.9 copy.115
  405.4 3.5 multiply_convert_fusion
  408.9 2.2 copy.120
  413.2 133.7 %reduce-scatter.4.cloned.1.call-done = f32[192,256]{1,0:T(8,128)} async-done(((f32[6144,256]{1,0:T(8,128)}), f32[192,256]{1,0:T(8,128)}) %reduce-scatter.4.cloned.1.call-update) | async-done | bytes 196624
  (66 shorter events, 34.4 us)
Async XLA Ops:
  7.2 85.7 %all-gather.11.cloned.1.call-start = ((), (), s32[]{:S(2)}) async-start(), calls=%async_computation.5 | async-start | bytes 3244032 | tf_op jit(solution)/shard_map/all_gather | solution.py:76
  7.9 119.3 %all-gather.13.cloned.1.call-start = ((), (), s32[]{:S(2)}) async-start(), calls=%async_computation.6 | async-start | bytes 5308416 | tf_op jit(solution)/shard_map/all_gather | solution.py:84
  8.7 201.6 %all-gather.7.cloned.1.call-start = ((), (), s32[]{:S(2)}) async-start(), calls=%async_computation.3 | async-start | bytes 3244032 | tf_op jit(solution)/shard_map/all_gather | solution.py:77
  9.4 235.0 %all-gather.9.cloned.1.call-start = ((), (), s32[]{:S(2)}) async-start(), calls=%async_computation.4 | async-start | bytes 5308416 | tf_op jit(solution)/shard_map/all_gather | solution.py:85
  10.0 350.0 %all-gather.15.cloned.1.call-start = ((), (), s32[]{:S(2)}) async-start(), calls=%async_computation.7 | async-start | bytes 1769472 | tf_op jit(solution)/shard_map/all_gather | solution.py:101
  250.3 140.2 %all-gather.17.cloned.1.call-start = ((), (), s32[]{:S(2)}) async-start(), calls=%async_computation.8 | async-start | bytes 1769472 | tf_op jit(solution)/shard_map/all_gather | solution.py:102
  250.9 296.1 %reduce-scatter.4.cloned.1.call-start = ((), (), s32[]{:S(2)}) async-start(), calls=%async_computation.9 | async-start | bytes 6488064
  264.5 1.9 copy-start
  316.1 41.0 %all-to-all-start.1 = ((bf16[256,8,768]{0,2,1:T(8,128)(2,1)}), bf16[256,8,768]{0,2,1:T(8,128)(2,1)S(1)}, u32[]{:S(2)}, u32[]{:S(2)}) async-start(bf16[256,8,768]{0,2,1:T(8,128)(2,1)} %bitcast.39), calls=%async_computation.1 | async-start | bytes 6291456 | tf_op jit(solution)/shard_map/all_to_all | solution.py:81
  320.2 4.3 copy-start.8
  325.5 2.7 copy-start.9
  332.0 4.3 copy-start.10
  337.4 2.7 copy-start.11
  370.4 1.6 copy-start.5
  384.0 6.5 %copy-start.1 = (bf16[8,256,768]{2,1,0:T(8,128)(2,1)S(1)}, bf16[8,256,768]{2,1,0:T(8,128)(2,1)}, u32[]{:S(2)}) copy-start(bf16[8,256,768]{2,1,0:T(8,128)(2,1)} %copy.109) | copy-start | bytes 9437188
  398.5 1.3 copy-start.4
  402.5 2.9 copy-start.2
  402.5 2.9 copy-start.3
  408.9 2.2 copy-start.7
  408.9 3.3 copy-start.6
Sparse Core Ops, SparseCore 0:
  10.6 82.2 all-gather.10
  94.7 32.4 all-gather.12
  129.8 80.3 all-gather.6
  211.9 32.4 all-gather.8
  250.4 27.9 all-gather.14
  280.1 34.5 all-gather.16
  318.7 228.2 reduce-scatter.3
where the time goes:
time: 557 us; the launch traced here: 556 us
  waiting for transfers between devices  370 us (66%)
  local copies, waits for them, and re-layouts  75.1 us (13%)
  blocking collectives  49.7 us (9%)
  matrix products  31.3 us (6%)
  between operations  14.2 us (3%)
  other arithmetic  11.2 us (2%)
    unnamed x8, waiting for transfers between devices  137 us
    all_gather x1, waiting for transfers between devices, local(): lax.all_gather(tokens, 'col', axis=1, tiled=True)  82.9 us
    all_gather x1, waiting for transfers between devices, local(): lax.all_gather(cotangent, 'col', axis=1, tiled=True)  77.2 us
    all_to_all x1, blocking collectives, local(): lax.all_to_all(token_rows, 'row', split_axis=1, concat_axis=0, tiled=True)  49.7 us
    unnamed x39, local copies, waits for them, and re-layouts  35.3 us
    all_gather x1, waiting for transfers between devices, local(): lax.all_gather(w_expand, 'row', axis=0, tiled=True)  34.3 us
    all_gather x1, waiting for transfers between devices, local(): lax.all_gather(w_reduce, 'row', axis=0, tiled=True)  34.2 us
    mul x16, local copies, waits for them, and re-layouts, spread_scale(): return (shaped * scale[:, None, :]).reshape(values.shape)  26.2 us
  transfers between devices with their start and end apart: 8, of which 6 were waited for; matrix products, arithmetic and copies ran while one was open for 19% of the time, Pallas kernels for 0%

commit v1 on v0

--- a/solution.py
+++ b/solution.py
@@ -10,6 +10,17 @@
 learn_rate = 0.001
 decay_rate = 0.1
 scale_eps = 1e-06
+
+
+def gather_around(array, axis, dim):
+    ways = lax.axis_size(axis)
+    pieces = [array]
+    for far in range(1, ways):
+        pieces.append(
+            lax.ppermute(pieces[far - 1], axis, [(d, (d - 1) % ways) for d in range(ways)])
+        )
+    line = jnp.concatenate(pieces, axis=dim)
+    return jnp.roll(line, lax.axis_index(axis) * array.shape[dim], axis=dim)
 
 
 def gelu_pair(pre_act):
@@ -82,7 +93,7 @@
     )
     up_panel, down_panel = (
         lax.all_gather(w_expand, "row", axis=0, tiled=True),
-        lax.all_gather(w_reduce, "row", axis=0, tiled=True),
+        gather_around(w_reduce, "row", 0),
     )
     pre_act = jnp.dot(token_rows, up_panel, preferred_element_type=jnp.float32)
     act_grad = jnp.dot(cot_rows, down_panel, preferred_element_type=jnp.float32)

time: 557 us -> 522 us (0.937)
  waiting for transfers between devices: 370 us -> 309 us
  local copies, waits for them, and re-layouts: 75.1 us -> 91.6 us
  starting transfers between devices: 4.3 us -> 17.7 us
    all_gather x1, waiting for transfers between devices: 82.9 us -> 9.41 us  [local(): lax.all_gather(tokens, 'col', axis=1, tiled=True)]
    ppermute x0 -> x7, waiting for transfers between devices: none -> 45.1 us  [gather_around(): lax.ppermute(pieces[far - 1], axis, [(d, (d - 1) % ways) for d in range(w...]
    all_gather x1 -> x0, waiting for transfers between devices: 34.2 us -> none  [local(): lax.all_gather(w_reduce, 'row', axis=0, tiled=True)]
    unnamed x39 -> x56, local copies, waits for them, and re-layouts: 35.3 us -> 50.8 us
    ppermute x0 -> x7, starting transfers between devices: none -> 12.5 us  [gather_around(): lax.ppermute(pieces[far - 1], axis, [(d, (d - 1) % ways) for d in range(w...]
    unnamed x8 -> x7, waiting for transfers between devices: 137 us -> 139 us
  transfers between devices with their start and end apart: 8 -> 14, of which waited for: 6 -> 12; matrix products, arithmetic and copies ran while one was open for 19% -> 24% of each run, Pallas kernels for 0% -> 0%
where the time goes in v1:
time: 522 us; the launch traced here: 521 us
  waiting for transfers between devices  309 us (59%)
  local copies, waits for them, and re-layouts  91.6 us (18%)
  blocking collectives  46.3 us (9%)
  matrix products  30.8 us (6%)
  starting transfers between devices  17.7 us (3%)
  between operations  14.2 us (3%)
  other arithmetic  11.2 us (2%)
    unnamed x7, waiting for transfers between devices  139 us
    all_gather x1, waiting for transfers between devices, local(): lax.all_gather(cotangent, 'col', axis=1, tiled=True)  77.1 us
    unnamed x56, local copies, waits for them, and re-layouts  50.8 us
    all_to_all x1, blocking collectives, local(): lax.all_to_all(token_rows, 'row', split_axis=1, concat_axis=0, tiled=True)  46.3 us
    ppermute x7, waiting for transfers between devices, gather_around(): lax.ppermute(pieces[far - 1], axis, [(d, (d - 1) % ways) for d in range(w...  45.1 us
    all_gather x1, waiting for transfers between devices, local(): lax.all_gather(w_expand, 'row', axis=0, tiled=True)  34.3 us
    mul x16, local copies, waits for them, and re-layouts, spread_scale(): return (shaped * scale[:, None, :]).reshape(values.shape)  26.3 us
    ppermute x7, starting transfers between devices, gather_around(): lax.ppermute(pieces[far - 1], axis, [(d, (d - 1) % ways) for d in range(w...  12.5 us
  transfers between devices with their start and end apart: 14, of which 12 were waited for; matrix products, arithmetic and copies ran while one was open for 24% of the time, Pallas kernels for 0%

profile of v1, /device:TPU:8, one launch (start us, length us, event | category | flops | bytes accessed | tf_op | source)
XLA Modules:
  0.0 520.9 jit_solution(13887255049499488872)
XLA Ops:
  9.5 7.7 %collective-permute-done = bf16[768,384]{1,0:T(8,128)(2,1)S(1)} collective-permute-done((bf16[768,384]{1,0:T(8,128)(2,1)}, bf16[768,384]{1,0:T(8,128)(2,1)S(1)}, u32[]{:S(2)}, u32[]{:S(2)}) %collective-permute-start) | collective-permute-done | bytes 589856 | tf_op jit(solution)/shard_map/ppermute | solution.py:20
  19.0 7.4 %collective-permute-done.1 = bf16[768,384]{1,0:T(8,128)(2,1)S(1)} collective-permute-done((bf16[768,384]{1,0:T(8,128)(2,1)S(1)}, bf16[768,384]{1,0:T(8,128)(2,1)S(1)}, u32[]{:S(2)}, u32[]{:S(2)}) %collective-permute-start.1) | collective-permute-done | bytes 589856 | tf_op jit(solution)/shard_map/ppermute | solution.py:20
  28.3 7.4 %collective-permute-done.2 = bf16[768,384]{1,0:T(8,128)(2,1)S(1)} collective-permute-done((bf16[768,384]{1,0:T(8,128)(2,1)S(1)}, bf16[768,384]{1,0:T(8,128)(2,1)S(1)}, u32[]{:S(2)}, u32[]{:S(2)}) %collective-permute-start.2) | collective-permute-done | bytes 589856 | tf_op jit(solution)/shard_map/ppermute | solution.py:20
  38.0 7.4 %collective-permute-done.3 = bf16[768,384]{1,0:T(8,128)(2,1)S(1)} collective-permute-done((bf16[768,384]{1,0:T(8,128)(2,1)S(1)}, bf16[768,384]{1,0:T(8,128)(2,1)S(1)}, u32[]{:S(2)}, u32[]{:S(2)}) %collective-permute-start.3) | collective-permute-done | bytes 589856 | tf_op jit(solution)/shard_map/ppermute | solution.py:20
  45.4 2.3 collective-permute-start.4
  47.7 7.4 %collective-permute-done.4 = bf16[768,384]{1,0:T(8,128)(2,1)S(1)} collective-permute-done((bf16[768,384]{1,0:T(8,128)(2,1)S(1)}, bf16[768,384]{1,0:T(8,128)(2,1)S(1)}, u32[]{:S(2)}, u32[]{:S(2)}) %collective-permute-start.4) | collective-permute-done | bytes 589856 | tf_op jit(solution)/shard_map/ppermute | solution.py:20
  58.8 5.6 %collective-permute-done.5 = bf16[768,384]{1,0:T(8,128)(2,1)} collective-permute-done((bf16[768,384]{1,0:T(8,128)(2,1)S(1)}, bf16[768,384]{1,0:T(8,128)(2,1)}, u32[]{:S(2)}, u32[]{:S(2)}) %collective-permute-start.5) | collective-permute-done | bytes 589856 | tf_op jit(solution)/shard_map/ppermute | solution.py:20
  64.4 2.3 collective-permute-start.6
  83.5 9.4 %all-gather.8.cloned.1.call-done = bf16[256,6144]{0,1:T(8,128)(2,1)} async-done(((bf16[256,192]{0,1:T(8,128)(2,1)}), bf16[256,6144]{0,1:T(8,128)(2,1)}) %all-gather.8.cloned.1.call-update) | async-done | bytes 3145744 | tf_op jit(solution)/shard_map/all_gather | solution.py:87
  92.9 34.3 %all-gather.10.cloned.1.call-done = bf16[6144,384]{1,0:T(8,128)(2,1)} async-done(((bf16[768,384]{1,0:T(8,128)(2,1)}), bf16[6144,384]{1,0:T(8,128)(2,1)}) %all-gather.10.cloned.1.call-update) | async-done | bytes 4718608 | tf_op jit(solution)/shard_map/all_gather | solution.py:95
  127.2 5.9 %multiply_convert_fusion.4 = (bf16[256,384]{0,1:T(8,128)(2,1)}, f32[256,384]{0,1:T(8,128)S(1)}) fusion(bf16[256,6144]{0,1:T(8,128)(2,1)} %all-gather.8.cloned.1.call-done, bf16[6144,384]{1,0:T(8,128)(2,1)} %all-gather.10.cloned.1.call-done), kind=kOutput, calls=%fused_computation.33 | convolution fusion | flops 1208451072 | bytes 8454144 | tf_op jit(solution)/shard_map/dot_general | solution.py:98
  133.2 77.1 %all-gather.6.cloned.1.call-done = bf16[256,6144]{0,1:T(8,128)(2,1)} async-done(((bf16[256,192]{0,1:T(8,128)(2,1)}), bf16[256,6144]{0,1:T(8,128)(2,1)}) %all-gather.6.cloned.1.call-update) | async-done | bytes 3145744 | tf_op jit(solution)/shard_map/all_gather | solution.py:88
  210.3 5.4 %fusion.16 = bf16[256,384]{0,1:T(8,128)(2,1)} fusion(bf16[256,6144]{0,1:T(8,128)(2,1)} %all-gather.6.cloned.1.call-done, bf16[12288,384]{1,0:T(8,128)(2,1)} %constant_dynamic-update-slice_fusion, s32[]{:T(128)S(6)} %select_n.14, f32[256,384]{0,1:T(8,128)S(1)} %get-tuple-element.82), kind=kOutput, calls=%fused_computation.27 | convolution fusion | flops 1208942592 | bytes 8454148 | tf_op jit(solution)/shard_map/dot_general | solution.py:99
  216.4 7.0 %convolution_bitcast_fusion = f32[6144,256]{0,1:T(8,128)} fusion(bf16[256,384]{0,1:T(8,128)(2,1)} %fusion.16, bf16[6144,384]{1,0:T(8,128)(2,1)} %all-gather.10.cloned.1.call-done), kind=kOutput, calls=%fused_computation | convolution fusion | flops 1207959552 | bytes 11206656 | tf_op jit(solution)/shard_map/dot_general | solution.py:104
  223.3 6.7 %copy.144 = f32[6144,256]{1,0:T(8,128)} copy(f32[6144,256]{0,1:T(8,128)} %convolution_bitcast_fusion) | data formatting | bytes 12582912
  231.9 46.3 %all_to_all.38 = bf16[256,8,768]{0,2,1:T(8,128)(2,1)} all-to-all(bf16[256,8,768]{0,2,1:T(8,128)(2,1)S(1)} %bitcast.60), channel_id=1, replica_groups=mesh['row'=8,'col'=32] {'row'}, dimensions={1} | all-to-all | bytes 6291456 | tf_op jit(solution)/shard_map/all_to_all | solution.py:91
  278.2 4.9 all-to-all-start.1
  288.6 2.7 copy.117
  292.5 2.7 copy.120
  300.5 2.7 copy.127
  304.4 2.7 copy.131
  311.3 4.7 copy.118
  316.0 4.1 all-to-all-done.1
  320.1 2.8 copy.129
  323.0 6.1 %fusion.29 = (f32[768,384]{0,1:T(8,128)}, f32[768,384]{0,1:T(8,128)S(1)}, f32[768,384]{0,1:T(8,128)S(1)}, f32[768,384]{0,1:T(8,128)S(1)}) fusion(f32[768,384]{0,1:T(8,128)} %copy.117, bf16[768,384]{0,1:T(8,128)(2,1)} %copy.116, f32[768,384]{0,1:T(8,128)} %copy.120, bf16[768,384]{0,1:T(8,128)(2,1)} %copy.119, ...), kind=kOutput, calls=%fused_computation.64 | convolution fusion | flops 1211793408 | bytes 12976128 | tf_op jit(solution)/shard_map/dot_general | solution.py:67
  329.1 2.7 copy.121
  340.7 2.7 copy.124
  343.4 3.5 multiply_convert_fusion.2
  353.4 6.3 %fusion.26 = (f32[768,384]{0,1:T(8,128)}, f32[768,384]{0,1:T(8,128)}, f32[768,384]{0,1:T(8,128)}, f32[768,384]{0,1:T(8,128)}) fusion(f32[768,384]{0,1:T(8,128)} %copy.127, bf16[768,384]{0,1:T(8,128)(2,1)} %copy.126, f32[768,384]{0,1:T(8,128)} %copy.131, bf16[768,384]{0,1:T(8,128)(2,1)} %copy.130, bf16[2048,384]{0,1:T(8,128)(2,1)} %all-gather.14.cloned.1.call-done, ...), kind=kOutput, calls=%fused_computation.62 | convolution fusion | flops 1211793408 | bytes 12976128 | tf_op jit(solution)/shard_map/dot_general | solution.py:67
  365.3 2.8 copy.135
  368.1 3.5 multiply_convert_fusion
  376.0 136.2 %reduce-scatter.4.cloned.1.call-done = f32[192,256]{1,0:T(8,128)} async-done(((f32[6144,256]{1,0:T(8,128)}), f32[192,256]{1,0:T(8,128)}) %reduce-scatter.4.cloned.1.call-update) | async-done | bytes 196624
  (95 shorter events, 75.6 us)
Async XLA Ops:
  7.2 49.8 %copy-start.4 = (bf16[768,384]{1,0:T(8,128)(2,1)S(1)}, bf16[768,384]{1,0:T(8,128)(2,1)}, u32[]{:S(2)}) copy-start(bf16[768,384]{1,0:T(8,128)(2,1)} %param.15) | copy-start | bytes 1769476
  7.2 85.7 %all-gather.8.cloned.1.call-start = ((), (), s32[]{:S(2)}) async-start(), calls=%async_computation.4 | async-start | bytes 3244032 | tf_op jit(solution)/shard_map/all_gather | solution.py:87
  7.9 119.3 %all-gather.10.cloned.1.call-start = ((), (), s32[]{:S(2)}) async-start(), calls=%async_computation.5 | async-start | bytes 5308416 | tf_op jit(solution)/shard_map/all_gather | solution.py:95
  8.7 201.6 %all-gather.6.cloned.1.call-start = ((), (), s32[]{:S(2)}) async-start(), calls=%async_computation.3 | async-start | bytes 3244032 | tf_op jit(solution)/shard_map/all_gather | solution.py:88
  9.4 313.6 %all-gather.12.cloned.1.call-start = ((), (), s32[]{:S(2)}) async-start(), calls=%async_computation.6 | async-start | bytes 1769472 | tf_op jit(solution)/shard_map/all_gather | solution.py:112
  9.5 7.7 %collective-permute-start = (bf16[768,384]{1,0:T(8,128)(2,1)}, bf16[768,384]{1,0:T(8,128)(2,1)S(1)}, u32[]{:S(2)}, u32[]{:S(2)}) collective-permute-start(bf16[768,384]{1,0:T(8,128)(2,1)} %param.15), channel_id=1, source_target_pairs={{0,224},{32,0},{64,32},{96,64},{128,96},{160,128},{192,160},{224,1... | collective-permute-start | bytes 1769480 | tf_op jit(solution)/shard_map/ppermute | solution.py:20
  17.2 9.2 %collective-permute-start.1 = (bf16[768,384]{1,0:T(8,128)(2,1)S(1)}, bf16[768,384]{1,0:T(8,128)(2,1)S(1)}, u32[]{:S(2)}, u32[]{:S(2)}) collective-permute-start(bf16[768,384]{1,0:T(8,128)(2,1)S(1)} %collective-permute-done), channel_id=1, source_target_pairs={{0,224},{32,0},{64,32},{96,64},{128,96},{160,128},{192,160},{224,1... | collective-permute-start | bytes 1769480 | tf_op jit(solution)/shard_map/ppermute | solution.py:20
  26.4 9.3 %collective-permute-start.2 = (bf16[768,384]{1,0:T(8,128)(2,1)S(1)}, bf16[768,384]{1,0:T(8,128)(2,1)S(1)}, u32[]{:S(2)}, u32[]{:S(2)}) collective-permute-start(bf16[768,384]{1,0:T(8,128)(2,1)S(1)} %collective-permute-done.1), channel_id=1, source_target_pairs={{0,224},{32,0},{64,32},{96,64},{128,96},{160,128},{192,160},{224,1... | collective-permute-start | bytes 1769480 | tf_op jit(solution)/shard_map/ppermute | solution.py:20
  35.7 9.7 %collective-permute-start.3 = (bf16[768,384]{1,0:T(8,128)(2,1)S(1)}, bf16[768,384]{1,0:T(8,128)(2,1)S(1)}, u32[]{:S(2)}, u32[]{:S(2)}) collective-permute-start(bf16[768,384]{1,0:T(8,128)(2,1)S(1)} %collective-permute-done.2), channel_id=1, source_target_pairs={{0,224},{32,0},{64,32},{96,64},{128,96},{160,128},{192,160},{224,1... | collective-permute-start | bytes 1769480 | tf_op jit(solution)/shard_map/ppermute | solution.py:20
  45.4 9.7 %collective-permute-start.4 = (bf16[768,384]{1,0:T(8,128)(2,1)S(1)}, bf16[768,384]{1,0:T(8,128)(2,1)S(1)}, u32[]{:S(2)}, u32[]{:S(2)}) collective-permute-start(bf16[768,384]{1,0:T(8,128)(2,1)S(1)} %collective-permute-done.3), channel_id=1, source_target_pairs={{0,224},{32,0},{64,32},{96,64},{128,96},{160,128},{192,160},{224,1... | collective-permute-start | bytes 1769480 | tf_op jit(solution)/shard_map/ppermute | solution.py:20
  55.1 9.3 %collective-permute-start.5 = (bf16[768,384]{1,0:T(8,128)(2,1)S(1)}, bf16[768,384]{1,0:T(8,128)(2,1)}, u32[]{:S(2)}, u32[]{:S(2)}) collective-permute-start(bf16[768,384]{1,0:T(8,128)(2,1)S(1)} %collective-permute-done.4), channel_id=1, source_target_pairs={{0,224},{32,0},{64,32},{96,64},{128,96},{160,128},{192,160},{224,1... | collective-permute-start | bytes 1769480 | tf_op jit(solution)/shard_map/ppermute | solution.py:20
  64.4 10.0 %collective-permute-start.6 = (bf16[768,384]{1,0:T(8,128)(2,1)}, bf16[768,384]{1,0:T(8,128)(2,1)S(1)}, u32[]{:S(2)}, u32[]{:S(2)}) collective-permute-start(bf16[768,384]{1,0:T(8,128)(2,1)} %collective-permute-done.5), channel_id=1, source_target_pairs={{0,224},{32,0},{64,32},{96,64},{128,96},{160,128},{192,160},{224,1... | collective-permute-start | bytes 1769480 | tf_op jit(solution)/shard_map/ppermute | solution.py:20
  215.7 137.7 %all-gather.14.cloned.1.call-start = ((), (), s32[]{:S(2)}) async-start(), calls=%async_computation.7 | async-start | bytes 1769472 | tf_op jit(solution)/shard_map/all_gather | solution.py:113
  216.3 295.9 %reduce-scatter.4.cloned.1.call-start = ((), (), s32[]{:S(2)}) async-start(), calls=%async_computation.8 | async-start | bytes 6488064
  230.0 1.9 copy-start.6
  278.2 41.9 %all-to-all-start.1 = ((bf16[256,8,768]{0,2,1:T(8,128)(2,1)}), bf16[256,8,768]{0,2,1:T(8,128)(2,1)S(1)}, u32[]{:S(2)}, u32[]{:S(2)}) async-start(bf16[256,8,768]{0,2,1:T(8,128)(2,1)} %bitcast.59), calls=%async_computation.1 | async-start | bytes 6291456 | tf_op jit(solution)/shard_map/all_to_all | solution.py:92
  283.2 4.3 copy-start.9
  288.6 2.7 copy-start.10
  295.2 4.3 copy-start.11
  300.5 2.7 copy-start.12
  333.2 1.6 copy-start.5
  346.9 6.5 %copy-start = (bf16[8,256,768]{2,1,0:T(8,128)(2,1)S(1)}, bf16[8,256,768]{2,1,0:T(8,128)(2,1)}, u32[]{:S(2)}) copy-start(bf16[8,256,768]{2,1,0:T(8,128)(2,1)} %copy.129) | copy-start | bytes 9437188
  361.4 1.3 copy-start.3
  365.3 2.8 copy-start.1
  365.3 2.8 copy-start.2
  371.7 2.2 copy-start.8
  371.7 3.3 copy-start.7
Sparse Core Ops, SparseCore 0:
  10.6 82.2 all-gather.7
  94.7 32.4 all-gather.9
  129.8 80.3 all-gather.5
  215.9 23.5 all-gather.11
  241.2 41.2 all-gather.13
  286.3 225.9 reduce-scatter.3
